TPU v7x, 32 devices: a whole 2x2x4 slice. The times are simulated.
32 devices in a mesh: ia: 4 (over z), ja: 4 (over y, x), ka: 2 (over core).
Axes of the slice: x: 2, y: 2, z: 4, core: 2. Of those that a mesh axis runs over, the one named last changes fastest.
Arguments:
- blocks: bfloat16 [4, 4, 4, 128, 128, 128], P('ia', 'ja', 'ka'), may hold values from -6 to 6
- coordinates: int32 [3, 4, 4, 4], P(None, 'ia', 'ja', 'ka'), may hold values from 0 to 3, as said below
- occupancy: int32 [4, 4, 4], P('ia', 'ja', 'ka'), may hold values from 0 to 1, as said below
- second_factor: bfloat16 [4, 512, 1024], P('ja', ('ia', 'ka')), may hold values from -12 to 12
- third_factor: bfloat16 [2, 512, 1024], P('ka', ('ia', 'ja')), may hold values from -0.0234375 to 0.0234375
- inverse_first: bfloat16 [1024, 1024], replicated
- inverse_second: bfloat16 [1024, 1024], replicated
Outputs:
- first_new: bfloat16 [4, 512, 1024], P('ia', ('ja', 'ka'))
- second_new: bfloat16 [4, 512, 1024], P('ja', ('ia', 'ka'))
Inputs may be any that keep to these rules, and one draw needn't show every extreme that they name: `occupancy`: each device has two slots; its second slot is occupied only where its first is. A device with two blocks is followed along ka, cyclically, by a device with none. Some device holds two blocks. coordinates[0], [1], [2] of a slot are a block row among 4, a block row among 4 and a block layer among 4 of its device's ranges; the two slots of a device name different layers.
All inputs are finite; a program needn't handle non-finite values.
Results may differ from a plain program's by a relative error of at most 0.006.
Values may be sent and summed in bfloat16 or wider, within the bound.
A program may use at most 128 MiB of HBM per device.

v0:
```python
import jax
import jax.numpy as jnp
from jax import lax
from jax.sharding import PartitionSpec as P

IB = 4
JB = 4


def passed_along(block, axis, distance):
    devices = range(lax.axis_size(axis))
    route = [((i - distance) % len(devices), i) for i in devices]
    return lax.ppermute(block, axis, route)


def block_products(tensor_block, left_rows, layer_slab, contract):
    block_edge = tensor_block.shape[0]
    step_rows = max(block_edge // 4, 1)
    summed = jnp.zeros((block_edge, left_rows.shape[1]), jnp.float32)
    for first_row in range(0, block_edge, step_rows):
        khatri = left_rows[first_row : first_row + step_rows][:, None, :] * layer_slab[None, :, :]
        if contract == 1:
            block_part = tensor_block[:, first_row : first_row + step_rows, :]
            contraction = (((1, 2), (0, 1)), ((), ()))
        else:
            block_part = tensor_block[first_row : first_row + step_rows]
            contraction = (((0, 2), (0, 1)), ((), ()))
        summed = summed + lax.dot_general(
            block_part, khatri, contraction, preferred_element_type=jnp.float32
        )
    return summed


def place_rows(partial_value, addend, block_index):
    block_edge = addend.shape[0]
    row_start = block_index * block_edge
    current = lax.dynamic_slice_in_dim(partial_value, row_start, block_edge, 0)
    return lax.dynamic_update_slice_in_dim(partial_value, addend, row_start, 0)


def pick_rows(source, block_index, block_edge):
    return lax.dynamic_slice_in_dim(source, block_index * block_edge, block_edge, 0)


def body(
    blocks, coordinates, occupancy, second_factor, third_factor, inverse_first, inverse_second
):
    block_edge = blocks.shape[-1]
    rank_width = inverse_first.shape[0]
    own_blocks = blocks.reshape(2, block_edge, block_edge, block_edge)
    places = coordinates.reshape(3, 2)
    occupied = occupancy.reshape(2)
    second_rows = lax.all_gather(second_factor, ("ia", "ka"), axis=1, tiled=True)[0]
    layer_rows = lax.all_gather(third_factor, ("ia", "ja"), axis=1, tiled=True)[0]
    slot_meta = jnp.stack([occupied[1], places[0, 1], places[1, 1]]).astype(jnp.bfloat16)
    arrived, arrived_layer, arrived_meta = passed_along(
        (own_blocks[1], pick_rows(layer_rows, places[2, 1], block_edge), slot_meta), "ka", 1
    )
    arrived_index = arrived_meta.astype(jnp.int32)
    keep_own = occupied[0] > 0
    tensor_block = jnp.where(keep_own, own_blocks[0], arrived)
    layer_slab = jnp.where(keep_own, pick_rows(layer_rows, places[2, 0], block_edge), arrived_layer)
    row_block = jnp.where(keep_own, places[0, 0], arrived_index[1])
    col_block = jnp.where(keep_own, places[1, 0], arrived_index[2])
    weight = jnp.where(keep_own, 1, arrived_index[0]).astype(jnp.float32)
    first_partial = jnp.zeros((IB * block_edge, rank_width), jnp.float32)
    contribution = block_products(
        tensor_block, pick_rows(second_rows, col_block, block_edge), layer_slab, 1
    )
    first_partial = place_rows(first_partial, contribution * weight, row_block)
    summed_rows = lax.psum(first_partial, ("ja", "ka"))
    first_rows = jnp.dot(
        summed_rows.astype(jnp.bfloat16), inverse_first, preferred_element_type=jnp.float32
    ).astype(jnp.bfloat16)
    share_rows = first_rows.shape[0] // lax.axis_size(("ja", "ka"))
    first_new = lax.dynamic_slice_in_dim(
        first_rows, lax.axis_index(("ja", "ka")) * share_rows, share_rows, 0
    )
    second_partial = jnp.zeros((JB * block_edge, rank_width), jnp.float32)
    contribution = block_products(
        tensor_block, pick_rows(first_rows, row_block, block_edge), layer_slab, 0
    )
    second_partial = place_rows(second_partial, contribution * weight, col_block)
    owned_second = lax.psum_scatter(
        second_partial[None], ("ia", "ka"), scatter_dimension=1, tiled=True
    )[0]
    second_new = jnp.dot(
        owned_second.astype(jnp.bfloat16), inverse_second, preferred_element_type=jnp.float32
    ).astype(jnp.bfloat16)
    return (first_new[None], second_new[None])


def solution(mesh):
    in_specs = (
        P("ia", "ja", "ka", None, None, None),
        P(None, "ia", "ja", "ka"),
        P("ia", "ja", "ka"),
        P("ja", ("ia", "ka"), None),
        P("ka", ("ia", "ja"), None),
        P(),
        P(),
    )
    out_specs = (P("ia", ("ja", "ka"), None), P("ja", ("ia", "ka"), None))
    return jax.shard_map(body, mesh=mesh, in_specs=in_specs, out_specs=out_specs, check_vma=False)
```

profile of v0, /device:TPU:0, one launch (start us, length us, event | category | flops | bytes accessed | tf_op | source)
XLA Modules:
  0.0 221.0 jit_solution(3574953310530504106)
XLA Ops:
  7.2 4.9 %slice_bitcast_fusion = bf16[128,128,128]{2,1,0:T(8,128)(2,1)} fusion(bf16[1,1,2,128,128,128]{5,4,3,2,1,0:T(8,128)(2,1)} %param.7), kind=kLoop, calls=%fused_computation.33 | loop fusion | bytes 8388608 | tf_op jit(solution)/shard_map/squeeze | solution.py:57
  12.1 0.5 collective-permute-start
  12.7 0.7 all-gather.3.cloned.1.call-update
  13.5 0.6 slice.105
  14.1 0.6 fusion.98
  15.4 0.7 fusion.100
  16.0 54.2 %all-gather.5.cloned.1.call-done = bf16[1,512,1024]{2,1,0:T(8,128)(2,1)} async-done(((bf16[1,32,1024]{2,1,0:T(8,128)(2,1)}), bf16[1,512,1024]{2,1,0:T(8,128)(2,1)}) %all-gather.5.cloned.1.call-update) | async-done | bytes 1048592 | tf_op jit(solution)/shard_map/all_gather | solution.py:54
  70.3 1.0 dynamic-slice_bitcast_fusion
  71.3 2.0 pad_maximum_fusion
  73.4 0.5 collective-permute-start.1
  74.7 0.7 fusion.99
  78.5 14.5 %all-gather.3.cloned.1.call-done = bf16[1,512,1024]{2,1,0:T(8,128)(2,1)} async-done(((bf16[1,64,1024]{2,1,0:T(8,128)(2,1)}), bf16[1,512,1024]{2,1,0:T(8,128)(2,1)}) %all-gather.3.cloned.1.call-update) | async-done | bytes 1048592 | tf_op jit(solution)/shard_map/all_gather | solution.py:53
  93.0 1.0 dynamic-slice_bitcast_fusion.5
  93.9 1.0 bitcast_select_fusion.1
  95.0 3.9 %bitcast_select_fusion = bf16[128,128,128]{2,1,0:T(8,128)(2,1)S(1)} fusion(bf16[128,128,128]{2,1,0:T(8,128)(2,1)} %collective-permute-done, bf16[1,1,2,128,128,128]{5,4,3,2,1,0:T(8,128)(2,1)} %param.7, pred[]{:T(512)} %bitcast), kind=kLoop, calls=%fused_computation.16 | loop fusion | flops 2097152 | bytes 12582913 | tf_op jit(solution)/shard_map/jit(_where)/select_n | solution.py:61
  98.9 0.8 fusion.97
  99.7 1.3 fusion.47
  101.0 1.3 fusion.50
  102.3 1.3 fusion.53
  103.7 1.6 broadcast.9
  105.3 2.1 fusion.86
  107.4 57.5 %all-reduce.1 = bf16[512,1024]{1,0:T(8,128)(2,1)S(1)} all-reduce(f32[512,1024]{1,0:T(8,128)} %fusion.86), channel_id=1, replica_groups=mesh['ia'=4,'ja'=4,'ka'=2] {'ja','ka'}, use_global_device_ids=true, to_apply=%region_0.1 | all-reduce | flops 524288 | bytes 3145728 | tf_op jit(solution)/shard_map/psum | solution.py:71
  164.9 1.3 convolution_convert_fusion
  166.2 1.0 copy-done.3
  167.2 2.6 %fusion.35 = f32[128,1024]{1,0:T(8,128)S(1)} fusion(bf16[128,128,128]{2,1,0:T(8,128)(2,1)} %copy-done.1, bf16[32,1024]{1,0:T(8,128)(2,1)S(1)} %get-tuple-element.8, bf16[128,1024]{1,0:T(8,128)(2,1)S(1)} %bitcast_select_fusion.1), kind=kOutput, calls=%fused_computation.36 | convolution fusion | flops 1090519040 | bytes 5046272 | tf_op jit(solution)/shard_map/dot_general | solution.py:28
  169.8 1.3 fusion.38
  171.2 1.3 fusion.41
  172.5 1.6 broadcast_in_dim.9
  174.1 2.3 %fusion.77 = f32[1,512,1024]{2,1,0:T(8,128)} fusion(f32[1,512,1024]{2,1,0:T(8,128)} %broadcast_in_dim.9, s32[]{:T(128)S(6)} %select_n.47, f32[128,1024]{1,0:T(8,128)S(1)} %fusion.41, f32[128,1024]{1,0:T(8,128)S(1)} %fusion.38, f32[128,1024]{1,0:T(8,128)S(1)} %fusion.35, bf16[128,128,128]{2,1,0:T(8,128)(2,1)S(1)} %copy-done.2, ...), kind=kOutput, calls=%fused_computation.50 | convolution fusion | flops 1091043328 | bytes 6619144 | tf_op jit(solution)/shard_map/dot_general | solution.py:28
  176.5 1.6 dynamic-slice_bitcast_fusion.1
  178.0 33.6 %reduce-scatter.2.cloned.1.call-done = f32[1,64,1024]{2,1,0:T(8,128)} async-done(((f32[1,512,1024]{2,1,0:T(8,128)}), f32[1,64,1024]{2,1,0:T(8,128)}) %reduce-scatter.2.cloned.1.call-update) | async-done | bytes 262160 | tf_op jit(solution)/shard_map/reduce_scatter | solution.py:84
  211.6 2.8 %fusion.89 = bf16[1,64,1024]{2,1,0:T(8,128)(2,1)} fusion(bf16[1024,1024]{1,0:T(8,128)(2,1)} %param.13, f32[1,64,1024]{2,1,0:T(8,128)} %reduce-scatter.2.cloned.1.call-done), kind=kOutput, calls=%fused_computation.55 | convolution fusion | flops 134348800 | bytes 2490368 | tf_op jit(solution)/shard_map/dot_general | solution.py:87
  (24 shorter events, 0.4 us)
Async XLA Ops:
  7.2 157.8 %copy-start = (bf16[1024,1024]{1,0:T(8,128)(2,1)S(1)}, bf16[1024,1024]{1,0:T(8,128)(2,1)}, u32[]{:S(2)}) copy-start(bf16[1024,1024]{1,0:T(8,128)(2,1)} %param.12) | copy-start | bytes 6291460
  7.2 6.3 %copy-start.5 = (s32[1,1,2]{2,1,0:T(1,128)S(1)}, s32[1,1,2]{2,1,0:T(1,128)}, u32[]{:S(2)}) copy-start(s32[1,1,2]{2,1,0:T(1,128)} %param.9) | copy-start | bytes 28
  7.2 6.9 %copy-start.4 = (s32[3,1,1,2]{0,3,2,1:T(2,128)S(1)}, s32[3,1,1,2]{0,3,2,1:T(2,128)}, u32[]{:S(2)}) copy-start(s32[3,1,1,2]{0,3,2,1:T(2,128)} %param.8) | copy-start | bytes 76
  7.2 63.1 %all-gather.5.cloned.1.call-start = ((), (), s32[]{:S(2)}) async-start(), calls=%async_computation.2 | async-start | bytes 1114112 | tf_op jit(solution)/shard_map/all_gather | solution.py:54
  12.1 82.9 %collective-permute-start = (bf16[128,128,128]{2,1,0:T(8,128)(2,1)}, bf16[128,128,128]{2,1,0:T(8,128)(2,1)}, u32[]{:S(2)}, u32[]{:S(2)}) collective-permute-start(bf16[128,128,128]{2,1,0:T(8,128)(2,1)} %slice_bitcast_fusion), channel_id=1, source_target_pairs={{1,0},{0,1},{3,2},{2,3},{5,4},{4,5},{7,6},{6,7},{9,8},{8,9},{11,10... | collective-permute-start | bytes 12582920 | tf_op jit(solution)/shard_map/ppermute | solution.py:13
  12.6 80.3 %all-gather.3.cloned.1.call-start = ((), (), s32[]{:S(2)}) async-start(), calls=%async_computation.1 | async-start | bytes 1179648 | tf_op jit(solution)/shard_map/all_gather | solution.py:53
  13.4 198.3 %reduce-scatter.2.cloned.1.call-start = ((), (), s32[]{:S(2)}) async-start(), calls=%async_computation.3 | async-start | bytes 2359296 | tf_op jit(solution)/shard_map/reduce_scatter | solution.py:84
  71.2 22.7 %collective-permute-start.2 = (bf16[128,1024]{1,0:T(8,128)(2,1)S(1)}, bf16[128,1024]{1,0:T(8,128)(2,1)S(1)}, u32[]{:S(2)}, u32[]{:S(2)}) collective-permute-start(bf16[128,1024]{1,0:T(8,128)(2,1)S(1)} %dynamic-slice_bitcast_fusion), channel_id=1, source_target_pairs={{1,0},{0,1},{3,2},{2,3},{5,4},{4,5},{7,6},{6,7},{9,8},{8,9},{11,10... | collective-permute-start | bytes 786440 | tf_op jit(solution)/shard_map/ppermute | solution.py:13
  73.4 1.3 collective-permute-start.1
  98.9 2.1 copy-start.1
  166.2 1.0 copy-start.3
  167.2 2.7 %copy-start.2 = (bf16[128,128,128]{2,1,0:T(8,128)(2,1)S(1)}, bf16[128,128,128]{2,1,0:T(8,128)(2,1)}, u32[]{:S(2)}) copy-start(bf16[128,128,128]{2,1,0:T(8,128)(2,1)} %copy-done.1) | copy-start | bytes 12582916
Sparse Core Ops, SparseCore 0:
  12.8 57.4 all-gather.4
  71.9 21.0 all-gather.2
  176.6 35.0 reduce-scatter.1
where the time goes:
time: 221 us
  waiting for transfers between devices  103 us (47%)
  blocking collectives  57.5 us (26%)
  between operations  18.5 us (8%)
  matrix products  17.8 us (8%)
  local copies, waits for them, and re-layouts  16 us (7%)
  other arithmetic  6.99 us (3%)
    psum x1, blocking collectives, body(): summed_rows = lax.psum(first_partial, ('ja', 'ka'))  57.5 us
    all_gather x1, waiting for transfers between devices, body(): lax.all_gather(third_factor, ('ia', 'ja'), axis=1, tiled=True)[0]  54.2 us
    reduce_scatter x1, waiting for transfers between devices, body(): lax.psum_scatter(second_partial[None], ('ia', 'ka'), scatter_dimension=1,...  33.6 us
    all_gather x1, waiting for transfers between devices, body(): lax.all_gather(second_factor, ('ia', 'ka'), axis=1, tiled=True)[0]  14.5 us
    dot_general x8, matrix products, block_products(): lax.dot_general(block_part, khatri, contraction, preferred_element_type=j...  13.7 us
    squeeze x1, local copies, waits for them, and re-layouts, body(): own_blocks[1]  4.87 us
  transfers between devices with their start and end apart: 6, of which 4 were waited for; matrix products, arithmetic and copies ran while one was open for 4% of the time, Pallas kernels for 0%

commit v1 on v0

--- a/solution.py
+++ b/solution.py
@@ -68,7 +68,8 @@
         tensor_block, pick_rows(second_rows, col_block, block_edge), layer_slab, 1
     )
     first_partial = place_rows(first_partial, contribution * weight, row_block)
-    summed_rows = lax.psum(first_partial, ("ja", "ka"))
+    parts = lax.all_gather(first_partial, ("ja", "ka"), axis=0, tiled=False)
+    summed_rows = parts.sum(axis=0)
     first_rows = jnp.dot(
         summed_rows.astype(jnp.bfloat16), inverse_first, preferred_element_type=jnp.float32
     ).astype(jnp.bfloat16)

time: 221 us -> 271 us (1.23)
  waiting for transfers between devices: 103 us -> 189 us
  blocking collectives: 57.5 us -> 0 us
  other arithmetic: 6.99 us -> 18.3 us
  local copies, waits for them, and re-layouts: 16 us -> 25 us
    all_gather x0 -> x1, waiting for transfers between devices: none -> 84.5 us  [body(): parts = lax.all_gather(first_partial, ('ja', 'ka'), axis=0, tiled=False)]
    psum x1 -> x0, blocking collectives: 57.5 us -> none  [body(): summed_rows = lax.psum(first_partial, ('ja', 'ka'))]
    slice x1 -> x2, local copies, waits for them, and re-layouts: 0.8 us -> 10 us  [the longest x1 5.35 us: body(): tensor_block = jnp.where(keep_own, own_blocks[0], arrived)]
    reduce_sum x0 -> x1, other arithmetic: none -> 7.94 us  [body(): summed_rows = parts.sum(axis=0)]
    squeeze x1 -> x0, local copies, waits for them, and re-layouts: 4.87 us -> none  [body(): own_blocks[1]]
    unnamed x12 -> x17, local copies, waits for them, and re-layouts: 0.99 us -> 5.67 us
    select_n x1, other arithmetic: 3.91 us -> 7.31 us  [body(): tensor_block = jnp.where(keep_own, own_blocks[0], arrived)]
    all_gather x0 -> x2, local copies, waits for them, and re-layouts: none -> 3.19 us  [body(): parts = lax.all_gather(first_partial, ('ja', 'ka'), axis=0, tiled=False)]
  transfers between devices with their start and end apart: 6 -> 7, of which waited for: 4 -> 5; matrix products, arithmetic and copies ran while one was open for 4% -> 5% of each run, Pallas kernels for 0% -> 0%
where the time goes in v1:
time: 271 us; the launch traced here: 270 us
  waiting for transfers between devices  189 us (70%)
  local copies, waits for them, and re-layouts  25 us (9%)
  between operations  18.5 us (7%)
  other arithmetic  18.3 us (7%)
  matrix products  18 us (7%)
    all_gather x1, waiting for transfers between devices, body(): parts = lax.all_gather(first_partial, ('ja', 'ka'), axis=0, tiled=False)  84.5 us
    all_gather x1, waiting for transfers between devices, body(): lax.all_gather(third_factor, ('ia', 'ja'), axis=1, tiled=True)[0]  54 us
    reduce_scatter x1, waiting for transfers between devices, body(): lax.psum_scatter(second_partial[None], ('ia', 'ka'), scatter_dimension=1,...  34.7 us
    all_gather x1, waiting for transfers between devices, body(): lax.all_gather(second_factor, ('ia', 'ka'), axis=1, tiled=True)[0]  14.5 us
    dot_general x8, matrix products, block_products(): lax.dot_general(block_part, khatri, contraction, preferred_element_type=j...  14 us
    reduce_sum x1, other arithmetic, body(): summed_rows = parts.sum(axis=0)  7.94 us
    select_n x1, other arithmetic, body(): tensor_block = jnp.where(keep_own, own_blocks[0], arrived)  7.31 us
    unnamed x17, local copies, waits for them, and re-layouts  5.67 us
  transfers between devices with their start and end apart: 7, of which 5 were waited for; matrix products, arithmetic and copies ran while one was open for 5% of the time, Pallas kernels for 0%

profile of v1, /device:TPU:0, one launch (start us, length us, event | category | flops | bytes accessed | tf_op | source)
XLA Modules:
  0.0 270.1 jit_solution(13673917645614490378)
XLA Ops:
  7.2 5.3 %fusion.101 = (bf16[1,1,1,128,128,128]{5,4,3,2,1,0:T(8,128)(2,1)}, bf16[1,1,1,128,128,128]{5,4,3,2,1,0:T(8,128)(2,1)S(1)}) fusion(bf16[1,1,2,128,128,128]{5,4,3,2,1,0:T(8,128)(2,1)} %param.7), kind=kLoop, calls=%fused_computation.78 | loop fusion | bytes 16777216 | tf_op jit(solution)/shard_map/slice | solution.py:61
  12.6 4.7 %copy.35 = bf16[1,1,1,128,128,128]{5,3,4,2,1,0:T(8,128)(2,1)} copy(bf16[1,1,1,128,128,128]{5,4,3,2,1,0:T(8,128)(2,1)S(1)} %get-tuple-element.3) | data formatting | bytes 8388608
  17.8 0.7 all-gather.4.cloned.1.call-update
  18.8 0.6 slice.105
  19.4 0.6 fusion.103
  20.7 0.7 fusion.105
  21.4 54.0 %all-gather.6.cloned.1.call-done = bf16[1,512,1024]{2,1,0:T(8,128)(2,1)} async-done(((bf16[1,32,1024]{2,1,0:T(8,128)(2,1)}), bf16[1,512,1024]{2,1,0:T(8,128)(2,1)}) %all-gather.6.cloned.1.call-update) | async-done | bytes 1048592 | tf_op jit(solution)/shard_map/all_gather | solution.py:54
  75.4 1.0 dynamic-slice_bitcast_fusion
  76.5 2.0 pad_maximum_fusion
  79.8 0.7 fusion.104
  83.7 14.5 %all-gather.4.cloned.1.call-done = bf16[1,512,1024]{2,1,0:T(8,128)(2,1)} async-done(((bf16[1,64,1024]{2,1,0:T(8,128)(2,1)}), bf16[1,512,1024]{2,1,0:T(8,128)(2,1)}) %all-gather.4.cloned.1.call-update) | async-done | bytes 1048592 | tf_op jit(solution)/shard_map/all_gather | solution.py:53
  98.1 1.0 dynamic-slice_bitcast_fusion.5
  99.1 1.0 bitcast_select_fusion
  100.1 7.3 %fusion.16 = bf16[128,128,128]{2,0,1:T(8,128)(2,1)S(1)} fusion(bf16[128,128,128]{2,0,1:T(8,128)(2,1)} %collective-permute-done, bf16[1,1,1,128,128,128]{5,4,3,2,1,0:T(8,128)(2,1)} %get-tuple-element.2, pred[]{:T(512)} %bitcast), kind=kLoop, calls=%fused_computation.18 | loop fusion | flops 2097152 | bytes 12582913 | tf_op jit(solution)/shard_map/jit(_where)/select_n | solution.py:61
  107.5 1.3 fusion.36
  108.8 1.3 fusion.39
  110.1 1.3 fusion.42
  111.5 1.6 all_gather.14.clone
  113.1 2.3 fusion.78
  115.7 4.7 %fusion.102 = (bf16[32,128,128]{2,0,1:T(8,128)(2,1)}, bf16[32,128,128]{2,0,1:T(8,128)(2,1)}, bf16[32,128,128]{2,0,1:T(8,128)(2,1)}, bf16[32,128,128]{2,0,1:T(8,128)(2,1)}) fusion(bf16[128,128,128]{2,0,1:T(8,128)(2,1)} %copy-done.1), kind=kLoop, calls=%fused_computation.79 | loop fusion | bytes 8388608 | tf_op jit(solution)/shard_map/slice | solution.py:26
  120.4 84.5 %all-gather.8.cloned.1.call-done = f32[8,512,1024]{2,1,0:T(8,128)} async-done(((f32[1,512,1024]{2,1,0:T(8,128)}), f32[8,512,1024]{2,1,0:T(8,128)}) %all-gather.8.cloned.1.call-update) | async-done | bytes 16777232 | tf_op jit(solution)/shard_map/all_gather | solution.py:71
  204.9 7.9 %reduce_sum.9 = bf16[512,1024]{1,0:T(8,128)(2,1)S(1)} reduce(f32[8,512,1024]{2,1,0:T(8,128)} %all-gather.8.cloned.1.call-done, f32[]{:T(128)} %constant.22.clone.1), dimensions={0}, to_apply=%region_0.1 | reduce | flops 3670016 | bytes 17825796 | tf_op jit(solution)/shard_map/reduce_sum | solution.py:72
  212.8 1.3 convolution_convert_fusion
  214.1 0.9 copy-done.5
  215.1 2.6 fusion.48
  217.7 1.4 fusion.51
  219.2 1.4 fusion.54
  220.6 1.6 all_gather.14
  222.2 2.2 fusion.90
  224.4 1.6 dynamic-slice_bitcast_fusion.1
  226.0 34.7 %reduce-scatter.2.cloned.1.call-done = f32[1,64,1024]{2,1,0:T(8,128)} async-done(((f32[1,512,1024]{2,1,0:T(8,128)}), f32[1,64,1024]{2,1,0:T(8,128)}) %reduce-scatter.2.cloned.1.call-update) | async-done | bytes 262160 | tf_op jit(solution)/shard_map/reduce_scatter | solution.py:85
  260.7 2.8 %fusion.93 = bf16[1,64,1024]{2,1,0:T(8,128)(2,1)} fusion(bf16[1024,1024]{1,0:T(8,128)(2,1)} %param.13, f32[1,64,1024]{2,1,0:T(8,128)} %reduce-scatter.2.cloned.1.call-done), kind=kOutput, calls=%fused_computation.57 | convolution fusion | flops 134348800 | bytes 2490368 | tf_op jit(solution)/shard_map/dot_general | solution.py:88
  (32 shorter events, 1.9 us)
Async XLA Ops:
  7.2 205.7 %copy-start = (bf16[1024,1024]{1,0:T(8,128)(2,1)S(1)}, bf16[1024,1024]{1,0:T(8,128)(2,1)}, u32[]{:S(2)}) copy-start(bf16[1024,1024]{1,0:T(8,128)(2,1)} %param.12) | copy-start | bytes 6291460
  7.2 68.2 %all-gather.6.cloned.1.call-start = ((), (), s32[]{:S(2)}) async-start(), calls=%async_computation.2 | async-start | bytes 1114112 | tf_op jit(solution)/shard_map/all_gather | solution.py:54
  12.6 6.2 %copy-start.7 = (s32[1,1,2]{2,1,0:T(1,128)S(1)}, s32[1,1,2]{2,1,0:T(1,128)}, u32[]{:S(2)}) copy-start(s32[1,1,2]{2,1,0:T(1,128)} %param.9) | copy-start | bytes 28
  12.6 6.8 %copy-start.6 = (s32[3,1,1,2]{0,3,2,1:T(2,128)S(1)}, s32[3,1,1,2]{0,3,2,1:T(2,128)}, u32[]{:S(2)}) copy-start(s32[3,1,1,2]{0,3,2,1:T(2,128)} %param.8) | copy-start | bytes 76
  17.3 82.9 %collective-permute-start = (bf16[128,128,128]{2,0,1:T(8,128)(2,1)}, bf16[128,128,128]{2,0,1:T(8,128)(2,1)}, u32[]{:S(2)}, u32[]{:S(2)}) collective-permute-start(bf16[128,128,128]{2,0,1:T(8,128)(2,1)} %bitcast.93), channel_id=1, source_target_pairs={{1,0},{0,1},{3,2},{2,3},{5,4},{4,5},{7,6},{6,7},{9,8},{8,9},{11,10... | collective-permute-start | bytes 12582920 | tf_op jit(solution)/shard_map/ppermute | solution.py:13
  17.8 80.3 %all-gather.4.cloned.1.call-start = ((), (), s32[]{:S(2)}) async-start(), calls=%async_computation.1 | async-start | bytes 1179648 | tf_op jit(solution)/shard_map/all_gather | solution.py:53
  18.5 186.3 %all-gather.8.cloned.1.call-start = ((), (), s32[]{:S(2)}) async-start(), calls=%async_computation.3 | async-start | bytes 18874368 | tf_op jit(solution)/shard_map/all_gather | solution.py:71
  76.4 22.7 %collective-permute-start.2 = (bf16[128,1024]{1,0:T(8,128)(2,1)S(1)}, bf16[128,1024]{1,0:T(8,128)(2,1)S(1)}, u32[]{:S(2)}, u32[]{:S(2)}) collective-permute-start(bf16[128,1024]{1,0:T(8,128)(2,1)S(1)} %dynamic-slice_bitcast_fusion), channel_id=1, source_target_pairs={{1,0},{0,1},{3,2},{2,3},{5,4},{4,5},{7,6},{6,7},{9,8},{8,9},{11,10... | collective-permute-start | bytes 786440 | tf_op jit(solution)/shard_map/ppermute | solution.py:13
  78.5 1.3 collective-permute-start.1
  107.4 5.6 %copy-start.1 = (bf16[128,128,128]{2,0,1:T(8,128)(2,1)}, bf16[128,128,128]{2,0,1:T(8,128)(2,1)S(1)}, u32[]{:S(2)}) copy-start(bf16[128,128,128]{2,0,1:T(8,128)(2,1)S(1)} %fusion.16) | copy-start | bytes 12582916
  115.4 145.3 %reduce-scatter.2.cloned.1.call-start = ((), (), s32[]{:S(2)}) async-start(), calls=%async_computation.4 | async-start | bytes 2359296 | tf_op jit(solution)/shard_map/reduce_scatter | solution.py:85
  214.1 1.0 copy-start.5
  215.1 2.6 copy-start.4
  217.7 1.4 copy-start.3
  219.2 3.0 %copy-start.2 = (bf16[32,128,128]{2,0,1:T(8,128)(2,1)S(1)}, bf16[32,128,128]{2,0,1:T(8,128)(2,1)}, u32[]{:S(2)}) copy-start(bf16[32,128,128]{2,0,1:T(8,128)(2,1)} %get-tuple-element.4) | copy-start | bytes 3145732
Sparse Core Ops, SparseCore 0:
  17.9 57.4 all-gather.5
  77.0 21.0 all-gather.3
  115.5 89.3 all-gather.7
  224.6 36.1 reduce-scatter.1
